TPU v7x, 32 devices: a whole 2x2x4 slice. The times are simulated.
32 devices in a mesh: edata: 4 (over z), expert: 8 (over y, x, core).
Axes of the slice: x: 2, y: 2, z: 4, core: 2. Of those that a mesh axis runs over, the one named last changes fastest.
Arguments:
- tokens: bfloat16 [1024, 4096], P('expert', 'edata'), may hold values from -6 to 6
- grad_out: bfloat16 [1024, 4096], P('expert', 'edata'), may hold values from -6 to 6
- expert_ids: int32 [1024, 8], P('expert'), may hold values from 0 to 15, all different within a row; in each aligned block of 128 rows (0 to 127, 128 to 255, ...) at most 80 rows name the same one
- route_prob: float32 [1024, 8], P('expert'), may hold values from 0.05 to 0.5
- w_gate: bfloat16 [16, 1024, 4096], P('expert', 'edata'), may hold values from -0.09375 to 0.09375
- w_up: bfloat16 [16, 1024, 4096], P('expert', 'edata'), may hold values from -0.09375 to 0.09375
- w_down: bfloat16 [16, 1024, 4096], P('expert', 'edata'), may hold values from -0.1875 to 0.1875
Outputs:
- grad_tokens: bfloat16 [1024, 4096], P('expert', 'edata')
- grad_gate: bfloat16 [16, 1024, 4096], P('expert', 'edata')
- grad_up: bfloat16 [16, 1024, 4096], P('expert', 'edata')
- grad_down: bfloat16 [16, 1024, 4096], P('expert', 'edata')
Inputs may be any that keep to these rules, and one draw needn't show every extreme that they name: `expert_ids`: each token names 8 different experts. Among the tokens of one aligned block of 128 no expert is named more than 80 times, and in every draw some expert is named exactly 80 times in some block.
All inputs are finite; a program needn't handle non-finite values.
Results may differ from a plain program's by a relative error of at most 0.012.
Values may be sent and summed in bfloat16 or wider, within the bound.
A program may use at most 192 MiB of HBM per device.

v0:
```python
import jax
import jax.numpy as jnp
from jax import lax
from jax.sharding import PartitionSpec as P


def ranks(onehot):
    pair_count = onehot.shape[-2]
    row = lax.broadcasted_iota(jnp.int32, (pair_count, pair_count), 0)
    col = lax.broadcasted_iota(jnp.int32, (pair_count, pair_count), 1)
    tri = (col < row).astype(jnp.bfloat16)
    earlier = jnp.einsum(
        "pq,...qe->...pe", tri, onehot.astype(jnp.bfloat16), preferred_element_type=jnp.float32
    )
    return earlier.astype(jnp.int32)


def body(tokens, grad_out, expert_ids, route_prob, w_gate, w_up, w_down):
    token_count, top_count = expert_ids.shape
    local_experts = w_gate.shape[0]
    expert_devices = lax.axis_size("expert")
    me = lax.axis_index("expert")
    experts_all = expert_devices * local_experts
    capacity = token_count * top_count * 5 // (4 * experts_all)
    pair_count = token_count * top_count
    cap_iota = jnp.arange(capacity, dtype=jnp.int32)
    routing = jnp.stack([expert_ids.astype(jnp.float32), route_prob])
    routing = lax.all_gather(routing, "expert", axis=1, tiled=False)
    all_ids, all_prob = (routing[0].astype(jnp.int32), routing[1])
    mine = me * local_experts + jnp.arange(local_experts, dtype=jnp.int32)
    named = all_ids.reshape(expert_devices, pair_count)[:, :, None] == mine
    rank = ranks(named)
    hit = named[..., None] & (rank[..., None] == cap_iota)
    hit = hit.reshape(expert_devices, token_count, top_count, local_experts, capacity)
    pick = jnp.sum(hit.astype(jnp.int32), 2).astype(jnp.bfloat16)
    prob_of = jnp.sum(jnp.where(hit, all_prob[:, :, :, None, None], 0.0), (1, 2))
    both = lax.all_gather(jnp.stack([tokens, grad_out]), "edata", axis=2, tiled=True)
    both = lax.all_gather(both, "expert", axis=1, tiled=False)
    all_x, all_dy = (both[0], both[1])
    slot_x = jnp.einsum("stxc,std->sxcd", pick, all_x, preferred_element_type=jnp.float32).astype(
        jnp.bfloat16
    )
    slot_dy = jnp.einsum("stxc,std->sxcd", pick, all_dy, preferred_element_type=jnp.float32)
    slot_dy = (prob_of[..., None] * slot_dy).astype(jnp.bfloat16)
    gate_value = jnp.einsum("sxcd,xfd->sxcf", slot_x, w_gate, preferred_element_type=jnp.float32)
    up_value = jnp.einsum("sxcd,xfd->sxcf", slot_x, w_up, preferred_element_type=jnp.float32)
    sigma = jax.nn.sigmoid(gate_value)
    active = gate_value * sigma
    hidden = (active * up_value).astype(jnp.bfloat16)
    back = jnp.einsum("sxcd,xfd->sxcf", slot_dy, w_down, preferred_element_type=jnp.float32)
    gate_grad = (back * up_value * sigma * (1.0 + gate_value * (1.0 - sigma))).astype(jnp.bfloat16)
    up_grad = (back * active).astype(jnp.bfloat16)
    grad_gate = jnp.einsum(
        "sxcf,sxcd->xfd", gate_grad, slot_x, preferred_element_type=jnp.float32
    ).astype(jnp.bfloat16)
    grad_up = jnp.einsum(
        "sxcf,sxcd->xfd", up_grad, slot_x, preferred_element_type=jnp.float32
    ).astype(jnp.bfloat16)
    grad_down = jnp.einsum(
        "sxcf,sxcd->xfd", hidden, slot_dy, preferred_element_type=jnp.float32
    ).astype(jnp.bfloat16)
    partial_value = jnp.einsum(
        "sxcf,xfd->sxcd", gate_grad, w_gate, preferred_element_type=jnp.float32
    )
    partial_value = partial_value + jnp.einsum(
        "sxcf,xfd->sxcd", up_grad, w_up, preferred_element_type=jnp.float32
    )
    partial_value = partial_value.astype(jnp.bfloat16)
    returned = lax.all_to_all(
        partial_value.reshape(expert_devices, local_experts * capacity, -1),
        "expert",
        split_axis=0,
        concat_axis=0,
        tiled=True,
    )
    width = returned.shape[-1]
    own = expert_ids.reshape(pair_count, 1) == jnp.arange(experts_all, dtype=jnp.int32)
    slot = jnp.sum(jnp.where(own, ranks(own), 0), 1)
    back_hit = own[:, :, None] & (slot[:, None, None] == cap_iota)
    gather_back = jnp.sum(
        back_hit.reshape(token_count, top_count, experts_all * capacity).astype(jnp.int32), 1
    ).astype(jnp.bfloat16)
    per_token = jnp.einsum(
        "tq,qd->td",
        gather_back,
        returned.reshape(experts_all * capacity, width),
        preferred_element_type=jnp.float32,
    )
    grad_tokens = lax.psum_scatter(per_token, "edata", scatter_dimension=1, tiled=True).astype(
        jnp.bfloat16
    )
    return (grad_tokens, grad_gate, grad_up, grad_down)


def solution(mesh):
    placed = (
        P("expert", "edata"),
        P("expert", "edata"),
        P("expert", None),
        P("expert", None),
        P("expert", "edata", None),
        P("expert", "edata", None),
        P("expert", "edata", None),
    )
    return jax.shard_map(
        body,
        mesh=mesh,
        in_specs=placed,
        out_specs=(
            P("expert", "edata"),
            P("expert", "edata", None),
            P("expert", "edata", None),
            P("expert", "edata", None),
        ),
        check_vma=False,
    )
```

profile of v0, /device:TPU:0, one launch (start us, length us, event | category | flops | bytes accessed | tf_op | source)
XLA Modules:
  0.0 408.3 jit_solution(9152429621475397026)
XLA Ops:
  7.2 0.0 all-gather.5.cloned.1.call-start
  7.2 1.9 pad_maximum_fusion
  9.1 0.0 all-gather.5.cloned.1.call-update
  9.1 0.0 all-gather.7.cloned.1.call-start
  9.2 49.4 %all-gather.5.cloned.1.call-done = bf16[2,128,4096]{2,1,0:T(8,128)(2,1)} async-done(((bf16[2,128,1024]{2,1,0:T(8,128)(2,1)}), bf16[2,128,4096]{2,1,0:T(8,128)(2,1)}) %all-gather.5.cloned.1.call-update) | async-done | bytes 2097168 | tf_op jit(solution)/shard_map/all_gather | solution.py:37
  58.5 0.0 all-gather.7.cloned.1.call-update
  58.6 0.7 convert_bitcast_fusion
  59.3 0.7 pad_maximum_fusion.1
  59.9 9.0 %all-gather = f32[2,1024,8]{1,2,0:T(8,128)S(1)} all-gather(f32[2,128,8]{1,2,0:T(8,128)S(1)} %pad_maximum_fusion.1), channel_id=2, replica_groups=mesh['edata'=4,'expert'=8] {'expert'}, dimensions={1}, use_global_device_ids=true | all-gather | bytes 73728 | tf_op jit(solution)/shard_map/all_gather | solution.py:28
  69.0 0.1 broadcast_compare_fusion
  69.1 0.2 copy.37
  69.3 0.3 convert_element_type.85
  69.6 0.5 fusion.49
  70.1 0.6 eq.89
  70.7 0.3 copy.38
  71.0 1.3 convert_reduce_fusion
  72.4 1.3 select_reduce_fusion
  73.7 75.3 %all-gather.7.cloned.1.call-done = bf16[2,1024,4096]{2,1,0:T(8,128)(2,1)} async-done(((bf16[2,128,4096]{2,1,0:T(8,128)(2,1)}), bf16[2,1024,4096]{2,1,0:T(8,128)(2,1)}) %all-gather.7.cloned.1.call-update) | async-done | bytes 16777232 | tf_op jit(solution)/shard_map/all_gather | solution.py:38
  149.0 9.5 %fusion.65 = (bf16[1,1024,4096]{2,1,0:T(8,128)(2,1)}, bf16[1,1024,4096]{2,1,0:T(8,128)(2,1)S(1)}) fusion(bf16[2,1024,4096]{2,1,0:T(8,128)(2,1)} %all-gather.7.cloned.1.call-done), kind=kLoop, calls=%fused_computation.65 | loop fusion | bytes 33554432 | tf_op jit(solution)/shard_map/slice | solution.py:39
  158.5 5.5 %convolution_convert_fusion = bf16[8,2,80,4096]{3,2,1,0:T(8,128)(2,1)} fusion(bf16[8,128,4096,1]{2,1,3,0:T(8,128)(2,1)S(1)} %bitcast.84, s32[8,128,2,80]{1,3,2,0:T(8,128)S(1)} %convert_reduce_fusion), kind=kOutput, calls=%fused_computation.11 | convolution fusion | flops 1347584000 | bytes 19529728 | tf_op jit(solution)/shard_map/stxc,std->sxcd/dot_general | solution.py:40
  163.9 0.0 slice-start
  163.9 9.3 %fusion.35 = f32[8,2,80,256]{3,2,0,1:T(8,128)} fusion(bf16[2,256,4096]{2,1,0:T(8,128)(2,1)} %param.11, bf16[8,2,80,4096]{3,2,1,0:T(8,128)(2,1)} %convolution_convert_fusion), kind=kOutput, calls=%fused_computation.35 | convolution fusion | flops 2684354560 | bytes 15990784 | tf_op jit(solution)/shard_map/sxcd,xfd->sxcf/dot_general | solution.py:45
  173.2 0.0 slice-start.1
  173.2 9.3 %fusion.30 = f32[8,2,80,256]{3,2,0,1:T(8,128)} fusion(bf16[2,256,4096]{2,1,0:T(8,128)(2,1)} %param.12, bf16[8,2,80,4096]{3,2,1,0:T(8,128)(2,1)} %convolution_convert_fusion), kind=kOutput, calls=%fused_computation.34 | convolution fusion | flops 2684354560 | bytes 15990784 | tf_op jit(solution)/shard_map/sxcd,xfd->sxcf/dot_general | solution.py:46
  182.5 0.0 slice-done
  182.5 0.0 slice-done.1
  182.5 5.4 %multiply_convert_fusion = bf16[8,2,80,4096]{3,2,1,0:T(8,128)(2,1)} fusion(f32[8,2,80]{2,1,0:T(2,128)S(1)} %select_reduce_fusion, bf16[8,128,4096,1]{2,1,3,0:T(8,128)(2,1)S(1)} %bitcast.87, s32[8,128,2,80]{1,3,2,0:T(8,128)S(1)} %convert_reduce_fusion), kind=kOutput, calls=%fused_computation.1 | convolution fusion | flops 1352826880 | bytes 19534848 | tf_op jit(solution)/shard_map/stxc,std->sxcd/dot_general | solution.py:43
  187.9 0.0 copy-start
  187.9 9.4 %multiply_convert_fusion.2 = (bf16[8,2,80,256]{3,2,0,1:T(8,128)(2,1)S(1)}, bf16[8,2,80,256]{3,2,0,1:T(8,128)(2,1)S(1)}) fusion(f32[8,2,80,256]{3,2,0,1:T(8,128)} %fusion.35, f32[8,2,80,256]{3,2,0,1:T(8,128)} %fusion.30, bf16[2,256,4096]{2,1,0:T(8,128)(2,1)} %param.13, bf16[8,2,80,4096]{3,2,1,0:T(8,128)(2,1)} %multiply_convert_fusion), kind=kOutput, calls=%fused_computation.38 | convolution fusion | flops 2688614400 | bytes 18612224 | tf_op jit(solution)/shard_map/sxcd,xfd->sxcf/dot_general | solution.py:50
  197.2 0.0 copy-done
  197.3 8.7 %fusion.20 = f32[2,8,80,4096]{3,2,1,0:T(8,128)} fusion(bf16[8,2,80,256]{3,2,0,1:T(8,128)(2,1)S(1)} %get-tuple-element.7, bf16[2,256,4096]{2,1,0:T(8,128)(2,1)S(1)} %copy-done), kind=kOutput, calls=%fused_computation.24 | convolution fusion | flops 2684354560 | bytes 25821184 | tf_op jit(solution)/shard_map/sxcf,xfd->sxcd/dot_general | solution.py:62
  206.0 13.0 %fusion = bf16[8,2,80,4096]{3,2,0,1:T(8,128)(2,1)} fusion(f32[2,8,80,4096]{3,2,1,0:T(8,128)} %fusion.20, bf16[8,2,80,256]{3,2,0,1:T(8,128)(2,1)S(1)} %get-tuple-element.6, bf16[2,256,4096]{2,1,0:T(8,128)(2,1)} %param.12), kind=kOutput, calls=%fused_computation.2 | convolution fusion | flops 2694840320 | bytes 36306944 | tf_op jit(solution)/shard_map/sxcf,xfd->sxcd/dot_general | solution.py:65
  219.0 9.4 %copy.42 = bf16[8,2,80,4096]{3,2,1,0:T(8,128)(2,1)} copy(bf16[8,2,80,4096]{3,2,0,1:T(8,128)(2,1)} %fusion) | data formatting | bytes 20971520 | tf_op jit(solution)/shard_map/convert_element_type | solution.py:68
  228.4 0.0 copy-start.1
  228.4 5.3 %all-to-all-start = ((bf16[8,160,4096]{2,1,0:T(8,128)(2,1)}), bf16[8,160,4096]{2,1,0:T(8,128)(2,1)}, u32[]{:S(2)}, u32[]{:S(2)}) async-start(bf16[8,160,4096]{2,1,0:T(8,128)(2,1)} %bitcast.83), calls=%async_computation | async-start | bytes 20971520 | tf_op jit(solution)/shard_map/all_to_all | solution.py:69
  233.7 0.0 reduce-scatter.2.cloned.1.call-start
  233.8 0.0 copy-done.1
  233.8 0.1 copy.34
  233.9 0.1 eq.76
  234.0 0.3 copy.35
  234.3 0.5 fusion.54
  234.8 0.2 iota_compare_fusion.9
  235.0 7.9 %and_convert_fusion = s32[1024,16,80]{2,1,0:T(8,128)} fusion(pred[1024,80]{1,0:T(8,128)(4,1)S(1)} %iota_compare_fusion.9, pred[1024,16]{1,0:T(8,128)(4,1)S(1)} %copy.35), kind=kLoop, calls=%fused_computation.10 | loop fusion | flops 2621440 | bytes 5341184 | tf_op jit(solution)/shard_map/convert_element_type | solution.py:81
  242.8 9.1 %reshape.90 = s32[128,8,1280]{2,1,0:T(8,128)} reshape(s32[1024,16,80]{2,1,0:T(8,128)} %and_convert_fusion) | data formatting | bytes 10485760 | tf_op jit(solution)/shard_map/convert_element_type | solution.py:81
  251.9 3.7 reduce_sum.37
  255.7 94.6 %all-to-all-done = bf16[8,160,4096]{2,1,0:T(8,128)(2,1)} async-done(((bf16[8,160,4096]{2,1,0:T(8,128)(2,1)}), bf16[8,160,4096]{2,1,0:T(8,128)(2,1)}, u32[]{:S(2)}, u32[]{:S(2)}) %all-to-all-start) | async-done | bytes 10485792 | tf_op jit(solution)/shard_map/all_to_all | solution.py:69
  350.2 6.8 %fusion.55 = f32[128,4096]{1,0:T(8,128)} fusion(bf16[1280,4096]{1,0:T(8,128)(2,1)} %bitcast.26, s32[128,1280]{1,0:T(8,128)S(1)} %reduce_sum.37), kind=kOutput, calls=%fused_computation.49 | convolution fusion | flops 1342341120 | bytes 13238272 | tf_op jit(solution)/shard_map/tq,qd->td/dot_general | solution.py:83
  357.1 0.0 reduce-scatter.2.cloned.1.call-update
  357.1 0.0 slice-start.2
  357.1 0.0 slice-start.3
  357.1 9.2 %bitcast_convert_fusion.1 = bf16[2,256,4096]{2,1,0:T(8,128)(2,1)} fusion(bf16[8,2,80,256]{3,2,0,1:T(8,128)(2,1)S(1)} %get-tuple-element.6, bf16[8,2,80,4096]{3,2,1,0:T(8,128)(2,1)} %convolution_convert_fusion), kind=kOutput, calls=%fused_computation.8 | convolution fusion | flops 2686451712 | bytes 15335424 | tf_op jit(solution)/shard_map/sxcf,sxcd->xfd/dot_general | solution.py:56
  366.3 0.0 slice-start.4
  366.3 0.0 copy-start.2
  366.3 0.0 copy-start.3
  366.3 9.3 %bitcast_convert_fusion.2 = bf16[2,256,4096]{2,1,0:T(8,128)(2,1)} fusion(bf16[8,2,80,256]{3,2,0,1:T(8,128)(2,1)S(1)} %get-tuple-element.7, bf16[8,2,80,4096]{3,2,1,0:T(8,128)(2,1)} %convolution_convert_fusion), kind=kOutput, calls=%fused_computation.9 | convolution fusion | flops 2686451712 | bytes 15335424 | tf_op jit(solution)/shard_map/sxcf,sxcd->xfd/dot_general | solution.py:53
  375.6 0.0 slice-done.2
  375.6 0.0 slice-done.3
  375.6 0.0 slice-done.4
  375.6 0.0 copy-done.2
  375.6 0.0 copy-done.3
  375.6 5.3 %bitcast_convert_fusion = bf16[2,256,4096]{2,1,0:T(8,128)(2,1)} fusion(bf16[8,2,80,4096]{3,2,1,0:T(8,128)(2,1)S(1)} %bitcast.89, f32[8,2,80,256]{3,2,0,1:T(8,128)S(1)} %copy-done.3, f32[8,2,80,256]{3,2,0,1:T(8,128)S(1)} %copy-done.2), kind=kOutput, calls=%fused_computation.7 | convolution fusion | flops 2688417792 | bytes 17301504 | tf_op jit(solution)/shard_map/sxcf,sxcd->xfd/dot_general | solution.py:59
  381.0 19.0 %reduce-scatter.2.cloned.1.call-done = f32[128,1024]{1,0:T(8,128)} async-done(((f32[128,4096]{1,0:T(8,128)}), f32[128,1024]{1,0:T(8,128)}) %reduce-scatter.2.cloned.1.call-update) | async-done | bytes 524304 | tf_op jit(solution)/shard_map/reduce_scatter | solution.py:89
  400.0 1.8 convert_element_type.96
  (6 shorter events, 0.1 us)
Async XLA Ops:
  7.2 51.4 %all-gather.5.cloned.1.call-start = ((), (), s32[]{:S(2)}) async-start(), calls=%async_computation.2 | async-start | bytes 2621440 | tf_op jit(solution)/shard_map/all_gather | solution.py:37
  9.1 139.9 %all-gather.7.cloned.1.call-start = ((), (), s32[]{:S(2)}) async-start(), calls=%async_computation.4 | async-start | bytes 18874368 | tf_op jit(solution)/shard_map/all_gather | solution.py:38
  163.9 18.6 %slice-start = ((s8[8388608]{0:T(1024)(128)(4,1)}), s8[4194304]{0:T(1024)(128)(4,1)S(1)}, s32[]{:S(2)}) async-start(s8[8388608]{0:T(1024)(128)(4,1)} %bitcast.85), calls=%async_computation.5 | async-start | bytes 8388608
  173.2 9.3 %slice-start.1 = ((s8[8388608]{0:T(1024)(128)(4,1)}), s8[4194304]{0:T(1024)(128)(4,1)S(1)}, s32[]{:S(2)}) async-start(s8[8388608]{0:T(1024)(128)(4,1)} %bitcast.85), calls=%async_computation.6 | async-start | bytes 8388608
  187.9 9.4 %copy-start = (bf16[2,256,4096]{2,1,0:T(8,128)(2,1)S(1)}, bf16[2,256,4096]{2,1,0:T(8,128)(2,1)}, u32[]{:S(2)}) copy-start(bf16[2,256,4096]{2,1,0:T(8,128)(2,1)} %param.11) | copy-start | bytes 12582916
  228.4 5.4 %copy-start.1 = (s32[128,8]{0,1:T(8,128)S(1)}, s32[128,8]{0,1:T(8,128)}, u32[]{:S(2)}) copy-start(s32[128,8]{0,1:T(8,128)} %param.9) | copy-start | bytes 12292
  228.4 121.8 %all-to-all-start = ((bf16[8,160,4096]{2,1,0:T(8,128)(2,1)}), bf16[8,160,4096]{2,1,0:T(8,128)(2,1)}, u32[]{:S(2)}, u32[]{:S(2)}) async-start(bf16[8,160,4096]{2,1,0:T(8,128)(2,1)} %bitcast.83), calls=%async_computation | async-start | bytes 20971520 | tf_op jit(solution)/shard_map/all_to_all | solution.py:69
  233.7 166.3 %reduce-scatter.2.cloned.1.call-start = ((), (), s32[]{:S(2)}) async-start(), calls=%async_computation.3 | async-start | bytes 2621440 | tf_op jit(solution)/shard_map/reduce_scatter | solution.py:89
  357.1 18.5 %slice-start.2 = ((s8[10485760]{0:T(1024)(128)(4,1)}), s8[4194304]{0:T(1024)(128)(4,1)S(1)}, s32[]{:S(2)}) async-start(s8[10485760]{0:T(1024)(128)(4,1)} %bitcast.88), calls=%async_computation.7 | async-start | bytes 8388608
  357.1 18.5 %slice-start.3 = ((s8[10485760]{0:T(1024)(128)(4,1)}), s8[4194304]{0:T(1024)(128)(4,1)S(1)}, s32[]{:S(2)}) async-start(s8[10485760]{0:T(1024)(128)(4,1)} %bitcast.88), calls=%async_computation.8 | async-start | bytes 8388608
  366.3 9.3 %slice-start.4 = ((s8[10485760]{0:T(1024)(128)(4,1)}), s8[2097152]{0:T(1024)(128)(4,1)S(1)}, s32[]{:S(2)}) async-start(s8[10485760]{0:T(1024)(128)(4,1)} %bitcast.88), calls=%async_computation.9 | async-start | bytes 4194304
  366.3 9.3 %copy-start.2 = (f32[8,2,80,256]{3,2,0,1:T(8,128)S(1)}, f32[8,2,80,256]{3,2,0,1:T(8,128)}, u32[]{:S(2)}) copy-start(f32[8,2,80,256]{3,2,0,1:T(8,128)} %fusion.35) | copy-start | bytes 3932164
  366.3 9.3 %copy-start.3 = (f32[8,2,80,256]{3,2,0,1:T(8,128)S(1)}, f32[8,2,80,256]{3,2,0,1:T(8,128)}, u32[]{:S(2)}) copy-start(f32[8,2,80,256]{3,2,0,1:T(8,128)} %fusion.30) | copy-start | bytes 3932164
Sparse Core Ops, SparseCore 0:
  10.1 48.3 all-gather.4
  60.4 88.5 all-gather.6
  357.2 42.7 reduce-scatter.1
where the time goes:
time: 409 us; the launch traced here: 408 us
  waiting for transfers between devices  238 us (58%)
  matrix products  92.1 us (23%)
  local copies, waits for them, and re-layouts  29.9 us (7%)
  other arithmetic  19.5 us (5%)
  between operations  13.9 us (3%)
  blocking collectives  9.03 us (2%)
  starting transfers between devices  5.41 us (1%)
    all_to_all x1, waiting for transfers between devices, body(): lax.all_to_all(partial_value.reshape(expert_devices, local_experts * capa...  94.6 us
    all_gather x1, waiting for transfers between devices, body(): both = lax.all_gather(both, 'expert', axis=1, tiled=False)  75.3 us
    all_gather x1, waiting for transfers between devices, body(): lax.all_gather(jnp.stack([tokens, grad_out]), 'edata', axis=2, tiled=True)  49.4 us
    reduce_scatter x1, waiting for transfers between devices, body(): lax.psum_scatter(per_token, 'edata', scatter_dimension=1, tiled=True)  19 us
    dot_general x1, matrix products, body(): jnp.einsum('sxcf,xfd->sxcd', up_grad, w_up, preferred_element_type=jnp.fl...  13 us
    slice x1, local copies, waits for them, and re-layouts, body(): all_x, all_dy = (both[0], both[1])  9.49 us
    convert_element_type x1, local copies, waits for them, and re-layouts, body(): partial_value = partial_value.astype(jnp.bfloat16)  9.44 us
    dot_general x1, matrix products, body(): jnp.einsum('sxcd,xfd->sxcf', slot_dy, w_down, preferred_element_type=jnp....  9.36 us
  transfers between devices with their start and end apart: 4, of which 4 were waited for; matrix products, arithmetic and copies ran while one was open for 13% of the time, Pallas kernels for 0%

commit v1 on v0

--- a/solution.py
+++ b/solution.py
@@ -1,7 +1,35 @@
+import functools
 import jax
 import jax.numpy as jnp
 from jax import lax
 from jax.sharding import PartitionSpec as P
+from jax.lax import axis_index, axis_size, ppermute
+
+
+def _make_waves(vector, device_axis):
+    known, view_out, f_now = (axis_size(device_axis), axis_index(device_axis), vector.shape[2])
+    table = [(i0, (i0 + 1) % known) for i0 in range(known)]
+    by_place = [(i0, (i0 - 1) % known) for i0 in range(known)]
+    later = jnp.zeros((*vector.shape[:2], known * f_now, *vector.shape[3:]), vector.dtype)
+    later = lax.dynamic_update_slice_in_dim(later, vector, view_out * f_now, axis=2)
+    x_new = frame_out = vector
+    step_out = known // 2
+    to_i = 1
+    while to_i < step_out + 1:
+        x_new = ppermute(x_new, device_axis, table)
+        later = lax.dynamic_update_slice_in_dim(
+            later, x_new, (view_out - to_i) % known * f_now, axis=2
+        )
+        if to_i < known - step_out:
+            frame_out = ppermute(frame_out, axis_name=device_axis, perm=by_place)
+            later = lax.dynamic_update_slice_in_dim(
+                later, frame_out, (view_out + to_i) % known * f_now, axis=2
+            )
+        to_i += 1
+    return later
+
+
+get_the_strings = functools.partial(_make_waves, device_axis="edata")
 
 
 def ranks(onehot):
@@ -34,7 +62,7 @@
     hit = hit.reshape(expert_devices, token_count, top_count, local_experts, capacity)
     pick = jnp.sum(hit.astype(jnp.int32), 2).astype(jnp.bfloat16)
     prob_of = jnp.sum(jnp.where(hit, all_prob[:, :, :, None, None], 0.0), (1, 2))
-    both = lax.all_gather(jnp.stack([tokens, grad_out]), "edata", axis=2, tiled=True)
+    both = get_the_strings(jnp.stack([tokens, grad_out]))
     both = lax.all_gather(both, "expert", axis=1, tiled=False)
     all_x, all_dy = (both[0], both[1])
     slot_x = jnp.einsum("stxc,std->sxcd", pick, all_x, preferred_element_type=jnp.float32).astype(

time: 409 us -> 395 us (0.966)
  waiting for transfers between devices: 238 us -> 221 us
  local copies, waits for them, and re-layouts: 29.9 us -> 24.2 us
  starting transfers between devices: 5.41 us -> 10.7 us
  matrix products: 92.1 us -> 97.1 us
    all_gather x1 -> x0, waiting for transfers between devices: 49.4 us -> none  [body(): lax.all_gather(jnp.stack([tokens, grad_out]), 'edata', axis=2, tiled=True)]
    ppermute x0 -> x3, waiting for transfers between devices: none -> 32 us  [the longest x2 23.3 us: _make_waves(): x_new = ppermute(x_new, device_axis, table)]
    slice x1 -> x0, local copies, waits for them, and re-layouts: 9.49 us -> none  [body(): all_x, all_dy = (both[0], both[1])]
    ppermute x0 -> x3, starting transfers between devices: none -> 5.2 us  [the longest x2 3.11 us: _make_waves(): x_new = ppermute(x_new, device_axis, table)]
    dot_general x1, matrix products: 5.46 us -> 10.2 us  [body(): jnp.einsum('stxc,std->sxcd', pick, all_x, preferred_element_type=jnp.floa...]
  transfers between devices with their start and end apart: 4 -> 6, of which waited for: 4 -> 6; matrix products, arithmetic and copies ran while one was open for 13% -> 13% of each run, Pallas kernels for 0% -> 0%
where the time goes in v1:
time: 395 us
  waiting for transfers between devices  221 us (56%)
  matrix products  97.1 us (25%)
  local copies, waits for them, and re-layouts  24.2 us (6%)
  other arithmetic  18.5 us (5%)
  between operations  14.3 us (4%)
  starting transfers between devices  10.7 us (3%)
  blocking collectives  9.1 us (2%)
    all_to_all x1, waiting for transfers between devices, body(): lax.all_to_all(partial_value.reshape(expert_devices, local_experts * capa...  94.4 us
    all_gather x1, waiting for transfers between devices, body(): both = lax.all_gather(both, 'expert', axis=1, tiled=False)  75.4 us
    ppermute x2, waiting for transfers between devices, _make_waves(): x_new = ppermute(x_new, device_axis, table)  23.3 us
    reduce_scatter x1, waiting for transfers between devices, body(): lax.psum_scatter(per_token, 'edata', scatter_dimension=1, tiled=True)  19 us
    dot_general x1, matrix products, body(): jnp.einsum('sxcf,xfd->sxcd', up_grad, w_up, preferred_element_type=jnp.fl...  13 us
    dot_general x1, matrix products, body(): jnp.einsum('stxc,std->sxcd', pick, all_x, preferred_element_type=jnp.floa...  10.2 us
    convert_element_type x1, local copies, waits for them, and re-layouts, body(): partial_value = partial_value.astype(jnp.bfloat16)  9.45 us
    dot_general x1, matrix products, body(): jnp.einsum('sxcd,xfd->sxcf', slot_dy, w_down, preferred_element_type=jnp....  9.36 us
  transfers between devices with their start and end apart: 6, of which 6 were waited for; matrix products, arithmetic and copies ran while one was open for 13% of the time, Pallas kernels for 0%

profile of v1, /device:TPU:0, one launch (start us, length us, event | category | flops | bytes accessed | tf_op | source)
XLA Modules:
  0.0 394.6 jit_solution(16731630980664390543)
XLA Ops:
  7.2 0.0 all-gather.3.cloned.1.call-start
  7.2 1.1 pad_maximum_fusion
  8.3 3.1 collective-permute-start
  11.4 2.1 collective-permute-start.1
  13.5 0.0 copy-start.3
  13.5 0.0 copy-start.4
  13.5 12.7 %collective-permute-done = bf16[2,128,1024]{2,1,0:T(8,128)(2,1)S(1)} collective-permute-done((bf16[2,128,1024]{2,1,0:T(8,128)(2,1)S(1)}, bf16[2,128,1024]{2,1,0:T(8,128)(2,1)S(1)}, u32[]{:S(2)}, u32[]{:S(2)}) %collective-permute-start) | collective-permute-done | bytes 524320 | tf_op jit(solution)/shard_map/ppermute | solution.py:19
  26.2 0.0 collective-permute-start.2
  26.2 0.2 all_gather.22
  26.5 1.1 bitcast_dynamic-update-slice_fusion.2
  27.7 8.7 %collective-permute-done.1 = bf16[2,128,1024]{2,1,0:T(8,128)(2,1)} collective-permute-done((bf16[2,128,1024]{2,1,0:T(8,128)(2,1)S(1)}, bf16[2,128,1024]{2,1,0:T(8,128)(2,1)}, u32[]{:S(2)}, u32[]{:S(2)}) %collective-permute-start.1) | collective-permute-done | bytes 524320 | tf_op jit(solution)/shard_map/ppermute | solution.py:24
  36.4 1.1 bitcast_dynamic-update-slice_fusion
  37.4 10.5 %collective-permute-done.2 = bf16[2,128,1024]{2,1,0:T(8,128)(2,1)} collective-permute-done((bf16[2,128,1024]{2,1,0:T(8,128)(2,1)S(1)}, bf16[2,128,1024]{2,1,0:T(8,128)(2,1)}, u32[]{:S(2)}, u32[]{:S(2)}) %collective-permute-start.2) | collective-permute-done | bytes 524320 | tf_op jit(solution)/shard_map/ppermute | solution.py:19
  48.0 1.1 bitcast_dynamic-update-slice_fusion.3
  49.1 0.0 copy-start.1
  49.1 1.3 copy-done.1
  50.4 0.0 all-gather.3.cloned.1.call-update
  50.4 0.0 copy-done.3
  50.4 0.0 copy-done.4
  50.4 9.1 %all-gather = f32[2,1024,8]{1,2,0:T(8,128)S(1)} all-gather(f32[2,128,8]{1,2,0:T(8,128)S(1)} %pad_maximum_fusion.1), channel_id=2, replica_groups=mesh['edata'=4,'expert'=8] {'expert'}, dimensions={1}, use_global_device_ids=true | all-gather | bytes 73728 | tf_op jit(solution)/shard_map/all_gather | solution.py:56
  59.6 0.1 broadcast_compare_fusion
  59.7 0.2 copy.43
  59.9 0.3 convert_element_type.85
  60.2 0.5 fusion.52
  60.7 0.6 eq.93
  61.3 0.3 copy.44
  61.6 1.3 convert_reduce_fusion
  62.9 1.3 select_reduce_fusion
  64.2 75.4 %all-gather.3.cloned.1.call-done = bf16[2,8,128,4096]{3,2,1,0:T(8,128)(2,1)} async-done(((bf16[2,1,128,4096]{3,2,1,0:T(8,128)(2,1)}), bf16[2,8,128,4096]{3,2,1,0:T(8,128)(2,1)}) %all-gather.3.cloned.1.call-update) | async-done | bytes 16777232 | tf_op jit(solution)/shard_map/all_gather | solution.py:66
  139.6 10.2 %fusion.7 = bf16[8,2,80,4096]{3,2,1,0:T(8,128)(2,1)} fusion(bf16[2,8,128,4096]{3,2,1,0:T(8,128)(2,1)} %all-gather.3.cloned.1.call-done, s32[8,128,2,80]{1,3,2,0:T(8,128)S(1)} %convert_reduce_fusion), kind=kOutput, calls=%fused_computation.15 | convolution fusion | flops 1347584000 | bytes 19529728 | tf_op jit(solution)/shard_map/stxc,std->sxcd/dot_general | solution.py:68
  149.8 9.3 %fusion.38 = f32[8,2,80,256]{3,2,0,1:T(8,128)} fusion(bf16[2,256,4096]{2,1,0:T(8,128)(2,1)} %param.11, bf16[8,2,80,4096]{3,2,1,0:T(8,128)(2,1)} %fusion.7), kind=kOutput, calls=%fused_computation.39 | convolution fusion | flops 2684354560 | bytes 15990784 | tf_op jit(solution)/shard_map/sxcd,xfd->sxcf/dot_general | solution.py:73
  159.1 0.0 copy-done
  159.1 6.3 %fusion.33 = f32[8,2,80,256]{3,2,0,1:T(8,128)} fusion(bf16[2,256,4096]{2,1,0:T(8,128)(2,1)} %param.12, bf16[8,2,80,4096]{3,2,1,0:T(8,128)(2,1)S(1)} %copy-done), kind=kOutput, calls=%fused_computation.38 | convolution fusion | flops 2684354560 | bytes 15990784 | tf_op jit(solution)/shard_map/sxcd,xfd->sxcf/dot_general | solution.py:74
  165.5 8.7 %multiply_convert_fusion = bf16[8,2,80,4096]{3,2,1,0:T(8,128)(2,1)} fusion(f32[8,2,80]{2,1,0:T(2,128)S(1)} %select_reduce_fusion, bf16[2,8,128,4096]{3,2,1,0:T(8,128)(2,1)} %all-gather.3.cloned.1.call-done, s32[8,128,2,80]{1,3,2,0:T(8,128)S(1)} %convert_reduce_fusion), kind=kOutput, calls=%fused_computation.1 | convolution fusion | flops 1352826880 | bytes 19534848 | tf_op jit(solution)/shard_map/stxc,std->sxcd/dot_general | solution.py:71
  174.2 9.4 %multiply_convert_fusion.2 = (bf16[8,2,80,256]{3,2,0,1:T(8,128)(2,1)S(1)}, bf16[8,2,80,256]{3,2,0,1:T(8,128)(2,1)S(1)}) fusion(f32[8,2,80,256]{3,2,0,1:T(8,128)} %fusion.38, f32[8,2,80,256]{3,2,0,1:T(8,128)} %fusion.33, bf16[2,256,4096]{2,1,0:T(8,128)(2,1)} %param.13, bf16[8,2,80,4096]{3,2,1,0:T(8,128)(2,1)} %multiply_convert_fusion), kind=kOutput, calls=%fused_computation.42 | convolution fusion | flops 2688614400 | bytes 18612224 | tf_op jit(solution)/shard_map/sxcd,xfd->sxcf/dot_general | solution.py:78
  183.6 0.0 copy-done.2
  183.6 8.5 %fusion.23 = f32[2,8,80,4096]{3,2,1,0:T(8,128)} fusion(bf16[8,2,80,256]{3,2,0,1:T(8,128)(2,1)S(1)} %get-tuple-element.5, bf16[2,256,4096]{2,1,0:T(8,128)(2,1)S(1)} %copy-done.2), kind=kOutput, calls=%fused_computation.28 | convolution fusion | flops 2684354560 | bytes 25821184 | tf_op jit(solution)/shard_map/sxcf,xfd->sxcd/dot_general | solution.py:90
  192.1 13.0 %fusion = bf16[8,2,80,4096]{3,2,0,1:T(8,128)(2,1)} fusion(f32[2,8,80,4096]{3,2,1,0:T(8,128)} %fusion.23, bf16[8,2,80,256]{3,2,0,1:T(8,128)(2,1)S(1)} %get-tuple-element.4, bf16[2,256,4096]{2,1,0:T(8,128)(2,1)} %param.12), kind=kOutput, calls=%fused_computation.2 | convolution fusion | flops 2694840320 | bytes 36306944 | tf_op jit(solution)/shard_map/sxcf,xfd->sxcd/dot_general | solution.py:93
  205.1 9.4 %copy.51 = bf16[8,2,80,4096]{3,2,1,0:T(8,128)(2,1)} copy(bf16[8,2,80,4096]{3,2,0,1:T(8,128)(2,1)} %fusion) | data formatting | bytes 20971520 | tf_op jit(solution)/shard_map/convert_element_type | solution.py:96
  214.5 5.2 %all-to-all-start = ((bf16[8,160,4096]{2,1,0:T(8,128)(2,1)}), bf16[8,160,4096]{2,1,0:T(8,128)(2,1)}, u32[]{:S(2)}, u32[]{:S(2)}) async-start(bf16[8,160,4096]{2,1,0:T(8,128)(2,1)} %bitcast.101), calls=%async_computation | async-start | bytes 20971520 | tf_op jit(solution)/shard_map/all_to_all | solution.py:97
  219.7 0.3 reduce-scatter.2.cloned.1.call-start
  220.0 0.1 copy.40
  220.1 0.1 eq.80
  220.2 0.3 copy.41
  220.5 0.5 fusion.57
  221.0 0.2 iota_compare_fusion.9
  221.2 7.9 %and_convert_fusion = s32[1024,16,80]{2,1,0:T(8,128)} fusion(pred[1024,80]{1,0:T(8,128)(4,1)S(1)} %iota_compare_fusion.9, pred[1024,16]{1,0:T(8,128)(4,1)S(1)} %copy.41), kind=kLoop, calls=%fused_computation.14 | loop fusion | flops 2621440 | bytes 5341184 | tf_op jit(solution)/shard_map/convert_element_type | solution.py:109
  229.1 9.1 %reshape.98 = s32[128,8,1280]{2,1,0:T(8,128)} reshape(s32[1024,16,80]{2,1,0:T(8,128)} %and_convert_fusion) | data formatting | bytes 10485760 | tf_op jit(solution)/shard_map/convert_element_type | solution.py:109
  238.1 3.7 reduce_sum.37
  241.9 94.4 %all-to-all-done = bf16[8,160,4096]{2,1,0:T(8,128)(2,1)} async-done(((bf16[8,160,4096]{2,1,0:T(8,128)(2,1)}), bf16[8,160,4096]{2,1,0:T(8,128)(2,1)}, u32[]{:S(2)}, u32[]{:S(2)}) %all-to-all-start) | async-done | bytes 10485792 | tf_op jit(solution)/shard_map/all_to_all | solution.py:97
  336.2 6.8 %fusion.58 = f32[128,4096]{1,0:T(8,128)} fusion(bf16[1280,4096]{1,0:T(8,128)(2,1)} %bitcast.33, s32[128,1280]{1,0:T(8,128)S(1)} %reduce_sum.37), kind=kOutput, calls=%fused_computation.57 | convolution fusion | flops 1342341120 | bytes 13238272 | tf_op jit(solution)/shard_map/tq,qd->td/dot_general | solution.py:111
  343.1 0.0 reduce-scatter.2.cloned.1.call-update
  343.1 0.0 slice-start
  343.1 0.0 slice-start.1
  343.1 9.2 %bitcast_convert_fusion.1 = bf16[2,256,4096]{2,1,0:T(8,128)(2,1)} fusion(bf16[8,2,80,256]{3,2,0,1:T(8,128)(2,1)S(1)} %get-tuple-element.4, bf16[8,2,80,4096]{3,2,1,0:T(8,128)(2,1)} %fusion.7), kind=kOutput, calls=%fused_computation.12 | convolution fusion | flops 2686451712 | bytes 15335424 | tf_op jit(solution)/shard_map/sxcf,sxcd->xfd/dot_general | solution.py:84
  352.3 9.3 %bitcast_convert_fusion.2 = bf16[2,256,4096]{2,1,0:T(8,128)(2,1)} fusion(bf16[8,2,80,256]{3,2,0,1:T(8,128)(2,1)S(1)} %get-tuple-element.5, bf16[8,2,80,4096]{3,2,1,0:T(8,128)(2,1)} %fusion.7), kind=kOutput, calls=%fused_computation.13 | convolution fusion | flops 2686451712 | bytes 15335424 | tf_op jit(solution)/shard_map/sxcf,sxcd->xfd/dot_general | solution.py:81
  361.6 0.0 slice-done
  361.6 0.0 slice-done.1
  361.6 0.0 slice-done.2
  361.6 0.0 copy-done.5
  361.6 0.0 copy-done.6
  361.6 5.3 %bitcast_convert_fusion = bf16[2,256,4096]{2,1,0:T(8,128)(2,1)} fusion(bf16[8,2,80,4096]{3,2,1,0:T(8,128)(2,1)S(1)} %bitcast.103, f32[8,2,80,256]{3,2,0,1:T(8,128)S(1)} %copy-done.6, f32[8,2,80,256]{3,2,0,1:T(8,128)S(1)} %copy-done.5), kind=kOutput, calls=%fused_computation.11 | convolution fusion | flops 2688417792 | bytes 17301504 | tf_op jit(solution)/shard_map/sxcf,sxcd->xfd/dot_general | solution.py:87
  367.0 19.0 %reduce-scatter.2.cloned.1.call-done = f32[128,1024]{1,0:T(8,128)} async-done(((f32[128,4096]{1,0:T(8,128)}), f32[128,1024]{1,0:T(8,128)}) %reduce-scatter.2.cloned.1.call-update) | async-done | bytes 524304 | tf_op jit(solution)/shard_map/reduce_scatter | solution.py:117
  386.0 1.8 convert_element_type.96
  (13 shorter events, 0.1 us)
Async XLA Ops:
  7.2 132.5 %all-gather.3.cloned.1.call-start = ((), (), s32[]{:S(2)}) async-start(), calls=%async_computation.2 | async-start | bytes 18874368 | tf_op jit(solution)/shard_map/all_gather | solution.py:66
  8.3 17.9 %collective-permute-start = (bf16[2,128,1024]{2,1,0:T(8,128)(2,1)S(1)}, bf16[2,128,1024]{2,1,0:T(8,128)(2,1)S(1)}, u32[]{:S(2)}, u32[]{:S(2)}) collective-permute-start(bf16[2,128,1024]{2,1,0:T(8,128)(2,1)S(1)} %pad_maximum_fusion), channel_id=1, source_target_pairs={{0,8},{8,16},{16,24},{24,0},{1,9},{9,17},{17,25},{25,1},{2,10},{10... | collective-permute-start | bytes 1572872 | tf_op jit(solution)/shard_map/ppermute | solution.py:19
  11.4 25.0 %collective-permute-start.1 = (bf16[2,128,1024]{2,1,0:T(8,128)(2,1)S(1)}, bf16[2,128,1024]{2,1,0:T(8,128)(2,1)}, u32[]{:S(2)}, u32[]{:S(2)}) collective-permute-start(bf16[2,128,1024]{2,1,0:T(8,128)(2,1)S(1)} %pad_maximum_fusion), channel_id=1, source_target_pairs={{0,24},{8,0},{16,8},{24,16},{1,25},{9,1},{17,9},{25,17},{2,26},{10... | collective-permute-start | bytes 1572872 | tf_op jit(solution)/shard_map/ppermute | solution.py:24
  13.5 36.9 %copy-start.3 = (s32[128,8]{0,1:T(8,128)S(1)}, s32[128,8]{0,1:T(8,128)}, u32[]{:S(2)}) copy-start(s32[128,8]{0,1:T(8,128)} %param.9) | copy-start | bytes 12292
  13.5 36.9 %copy-start.4 = (f32[128,8]{0,1:T(8,128)S(1)}, f32[128,8]{0,1:T(8,128)}, u32[]{:S(2)}) copy-start(f32[128,8]{0,1:T(8,128)} %param.10) | copy-start | bytes 12292
  26.2 21.7 %collective-permute-start.2 = (bf16[2,128,1024]{2,1,0:T(8,128)(2,1)S(1)}, bf16[2,128,1024]{2,1,0:T(8,128)(2,1)}, u32[]{:S(2)}, u32[]{:S(2)}) collective-permute-start(bf16[2,128,1024]{2,1,0:T(8,128)(2,1)S(1)} %collective-permute-done), channel_id=1, source_target_pairs={{0,8},{8,16},{16,24},{24,0},{1,9},{9,17},{17,25},{25,1},{2,10},{10... | collective-permute-start | bytes 1572872 | tf_op jit(solution)/shard_map/ppermute | solution.py:19
  49.1 1.3 copy-start.1
  149.8 9.3 %copy-start = (bf16[8,2,80,4096]{3,2,1,0:T(8,128)(2,1)S(1)}, bf16[8,2,80,4096]{3,2,1,0:T(8,128)(2,1)}, u32[]{:S(2)}) copy-start(bf16[8,2,80,4096]{3,2,1,0:T(8,128)(2,1)} %fusion.7) | copy-start | bytes 31457284
  174.2 9.4 %copy-start.2 = (bf16[2,256,4096]{2,1,0:T(8,128)(2,1)S(1)}, bf16[2,256,4096]{2,1,0:T(8,128)(2,1)}, u32[]{:S(2)}) copy-start(bf16[2,256,4096]{2,1,0:T(8,128)(2,1)} %param.11) | copy-start | bytes 12582916
  214.5 121.7 %all-to-all-start = ((bf16[8,160,4096]{2,1,0:T(8,128)(2,1)}), bf16[8,160,4096]{2,1,0:T(8,128)(2,1)}, u32[]{:S(2)}, u32[]{:S(2)}) async-start(bf16[8,160,4096]{2,1,0:T(8,128)(2,1)} %bitcast.101), calls=%async_computation | async-start | bytes 20971520 | tf_op jit(solution)/shard_map/all_to_all | solution.py:97
  219.7 166.3 %reduce-scatter.2.cloned.1.call-start = ((), (), s32[]{:S(2)}) async-start(), calls=%async_computation.3 | async-start | bytes 2621440 | tf_op jit(solution)/shard_map/reduce_scatter | solution.py:117
  343.1 18.5 %slice-start = ((s8[10485760]{0:T(1024)(128)(4,1)}), s8[4194304]{0:T(1024)(128)(4,1)S(1)}, s32[]{:S(2)}) async-start(s8[10485760]{0:T(1024)(128)(4,1)} %bitcast.102), calls=%async_computation.4 | async-start | bytes 8388608
  343.1 18.5 %slice-start.1 = ((s8[10485760]{0:T(1024)(128)(4,1)}), s8[4194304]{0:T(1024)(128)(4,1)S(1)}, s32[]{:S(2)}) async-start(s8[10485760]{0:T(1024)(128)(4,1)} %bitcast.102), calls=%async_computation.5 | async-start | bytes 8388608
  352.3 9.3 %slice-start.2 = ((s8[10485760]{0:T(1024)(128)(4,1)}), s8[2097152]{0:T(1024)(128)(4,1)S(1)}, s32[]{:S(2)}) async-start(s8[10485760]{0:T(1024)(128)(4,1)} %bitcast.102), calls=%async_computation.6 | async-start | bytes 4194304
  352.3 9.3 %copy-start.5 = (f32[8,2,80,256]{3,2,0,1:T(8,128)S(1)}, f32[8,2,80,256]{3,2,0,1:T(8,128)}, u32[]{:S(2)}) copy-start(f32[8,2,80,256]{3,2,0,1:T(8,128)} %fusion.38) | copy-start | bytes 3932164
  352.3 9.3 %copy-start.6 = (f32[8,2,80,256]{3,2,0,1:T(8,128)S(1)}, f32[8,2,80,256]{3,2,0,1:T(8,128)}, u32[]{:S(2)}) copy-start(f32[8,2,80,256]{3,2,0,1:T(8,128)} %fusion.33) | copy-start | bytes 3932164
Sparse Core Ops, SparseCore 0:
  50.5 89.0 all-gather.2
  343.2 42.7 reduce-scatter.1
